TPU v7x, 32 devices: a whole 2x2x4 slice. The times are simulated.
32 devices in a mesh: dp: 8 (over z, y), mp: 4 (over x, core).
Axes of the slice: x: 2, y: 2, z: 4, core: 2. Of those that a mesh axis runs over, the one named last changes fastest.
Arguments:
- hidden: bfloat16 [8192, 5120], P('dp'), may hold values from -6 to 6
- exit_depth: int32 [8192], P('dp'), may hold values from 0 to 3, as said below
- seq_ids: int32 [8192], P('dp'), may hold values from 0 to 3, as said below
- dest: int32 [8192], P('dp'), may hold values from 0 to 7, as said below
- norm_gain: bfloat16 [5120], replicated, may hold values from 0.5 to 1.5
- w_query: bfloat16 [5120, 3072], P(None, 'mp'), may hold values from -4 to 4
- w_key: bfloat16 [5120, 3072], P(None, 'mp'), may hold values from -4 to 4
- w_value: bfloat16 [5120, 3072], P(None, 'mp'), may hold values from -0.078125 to 0.078125
- w_out: bfloat16 [3072, 5120], P('mp'), may hold values from -0.4375 to 0.4375
Outputs:
- next_rows: bfloat16 [6144, 5120], P('dp', 'mp')
Inputs may be any that keep to these rules, and one draw needn't show every extreme that they name: exit_depth is 3 for at most 768 tokens of one sequence, and for exactly that many in some sequence. seq_ids never fall along a sequence. `dest`: within one sequence, at most 96 tokens with exit depth 3 name the same destination, and some sequence has exactly 96 that do.
All inputs are finite; a program needn't handle non-finite values.
Results may differ from a plain program's by a relative error of at most 0.014.
Values may be sent and summed in bfloat16 or wider, within the bound.
A program may use at most 128 MiB of HBM per device.

v0:
```python
import math

import jax
import jax.numpy as jnp
from jax import lax
from jax.sharding import PartitionSpec as P

HD = 128


def rotate_pairs(values, places):
    half_width = values.shape[-1] // 2
    frequency = 10000.0 ** (-jnp.arange(half_width, dtype=jnp.float32) / half_width)
    angle = places[:, None] * frequency[None, :]
    cosine = jnp.cos(angle)[:, None, :]
    sine_term = jnp.sin(angle)[:, None, :]
    first = values[..., :half_width]
    second = values[..., half_width:]
    return jnp.concatenate(
        [first * cosine - second * sine_term, second * cosine + first * sine_term], axis=-1
    )


def body(hidden, exit_depth, seq_ids, dest, norm_gain, w_query, w_key, w_value, w_out):
    peers = lax.axis_size("dp")
    groups = lax.axis_size("mp")
    tokens = hidden.shape[0]
    width = hidden.shape[1]
    slots = 3 * tokens // 4
    capacity = slots // peers
    feature_slice = width // groups
    scale_factor = 1.0 / math.sqrt(HD)
    widened = hidden.astype(jnp.float32)
    mean_square = jnp.mean(widened * widened, axis=-1, keepdims=True)
    normed = (widened * lax.rsqrt(mean_square + 1e-05) * norm_gain.astype(jnp.float32)).astype(
        jnp.bfloat16
    )
    row_index = jnp.arange(tokens, dtype=jnp.int32)
    places = row_index.astype(jnp.float32)
    keys = jnp.dot(normed, w_key, preferred_element_type=jnp.float32).reshape(tokens, -1, HD)
    keys = rotate_pairs(keys, places).astype(jnp.bfloat16)
    values = (
        jnp.dot(normed, w_value, preferred_element_type=jnp.float32)
        .astype(jnp.bfloat16)
        .reshape(tokens, -1, HD)
    )
    active = exit_depth == 3
    chosen = (
        (dest[:, None] == jnp.arange(peers, dtype=jnp.int32)[None, :]) & active[:, None]
    ).astype(jnp.int32)
    running = jnp.cumsum(chosen, axis=0)
    order_rank = jnp.sum(running * chosen, axis=1) - 1
    slot_of = jnp.where(active, dest * capacity + order_rank, slots)
    index_buffer = jnp.full((slots,), tokens, jnp.int32).at[slot_of].set(row_index, mode="drop")
    filled = index_buffer < tokens
    picked = jnp.minimum(index_buffer, tokens - 1)
    queries = jnp.dot(normed[picked], w_query, preferred_element_type=jnp.float32).reshape(
        slots, -1, HD
    )
    queries = rotate_pairs(queries, picked.astype(jnp.float32)).astype(jnp.bfloat16)
    scores = (
        jnp.einsum("qhd,khd->hqk", queries, keys, preferred_element_type=jnp.float32) * scale_factor
    )
    allowed = (seq_ids[picked][:, None] == seq_ids[None, :]) & (
        row_index[None, :] <= picked[:, None]
    )
    scores = jnp.where(allowed[None], scores, -1e30)
    highest = jnp.max(scores, axis=-1, keepdims=True)
    raised = jnp.exp(scores - highest)
    probs = (raised / jnp.sum(raised, axis=-1, keepdims=True)).astype(jnp.bfloat16)
    attended = jnp.einsum("hqk,khd->qhd", probs, values, preferred_element_type=jnp.float32)
    attended = attended.astype(jnp.bfloat16).reshape(slots, -1)
    partial_value = jnp.dot(attended, w_out, preferred_element_type=jnp.float32)
    partial_value = jnp.where(filled[:, None], partial_value, 0.0).astype(jnp.bfloat16)
    residual_rows = jnp.where(filled[:, None], hidden[picked], jnp.zeros((), jnp.bfloat16))
    own_features = lax.dynamic_slice_in_dim(
        residual_rows, lax.axis_index("mp") * feature_slice, feature_slice, 1
    )
    summed = lax.psum_scatter(partial_value, "mp", scatter_dimension=1, tiled=True).astype(
        jnp.float32
    )
    updated = (own_features.astype(jnp.float32) + summed).astype(jnp.bfloat16)
    result = lax.all_to_all(updated, "dp", split_axis=0, concat_axis=0, tiled=True)
    return result


def solution(mesh):
    return jax.shard_map(
        body,
        mesh=mesh,
        in_specs=(
            P("dp", None),
            P("dp"),
            P("dp"),
            P("dp"),
            P(),
            P(None, "mp"),
            P(None, "mp"),
            P(None, "mp"),
            P("mp", None),
        ),
        out_specs=P("dp", "mp"),
        check_vma=False,
    )
```

profile of v0, /device:TPU:0, one launch (start us, length us, event | category | flops | bytes accessed | tf_op | source)
XLA Modules:
  0.0 286.0 jit_solution(1246825872194328064)
XLA Ops:
  6.5 0.0 reduce-scatter.2.cloned.1.call-start
  6.5 0.7 fusion.42
  7.2 0.7 broadcast_compare_fusion
  7.9 0.7 fusion.18
  8.6 2.3 reduce-window.6
  10.9 0.3 slice_reduce_fusion
  11.2 0.2 reduce-window.9
  11.3 0.1 add_bitcast_fusion
  11.4 0.7 fusion.15
  12.1 0.7 compare_select_fusion.1
  12.8 4.3 %scatter_custom_fusion = s32[768]{0:T(1024)S(1)} fusion(s32[1024]{0:T(1024)S(1)} %compare_select_fusion.1, s32[1024]{0:T(1024)S(1)} %iota.42, s32[]{:T(128)} %constant.19.clone.1), kind=kCustom, calls=%fused_computation.55 | custom fusion | bytes 3076 | tf_op jit(solution)/shard_map/scatter | solution.py:54
  17.2 0.7 convert_element_type.59
  17.9 0.0 copy-start.1
  17.9 6.2 %fusion.1 = f32[1024]{0:T(1024)S(1)} fusion(bf16[1024,5120]{1,0:T(8,128)(2,1)} %param.9), kind=kLoop, calls=%fused_computation.7 | loop fusion | flops 15727616 | bytes 10489856 | tf_op jit(solution)/shard_map/reduce_sum | solution.py:34
  24.1 0.7 copy-done.1
  24.9 6.1 %fusion.3 = bf16[1024,5120]{1,0:T(8,128)(2,1)} fusion(bf16[1024,5120]{1,0:T(8,128)(2,1)S(1)} %copy-done.1, f32[5120]{0:T(1024)S(1)} %convert_element_type.59, f32[1024]{0:T(1024)S(1)} %add_rsqrt_fusion), kind=kLoop, calls=%fused_computation.9 | loop fusion | flops 20971520 | bytes 20996096 | tf_op jit(solution)/shard_map/convert_element_type | solution.py:35
  30.9 14.2 %convolution_convert_fusion = bf16[1024,768]{0,1:T(8,128)(2,1)} fusion(bf16[1024,5120]{1,0:T(8,128)(2,1)} %fusion.3, bf16[5120,768]{1,0:T(8,128)(2,1)} %param.16), kind=kOutput, calls=%fused_computation.28 | convolution fusion | flops 8053850112 | bytes 19922944 | tf_op jit(solution)/shard_map/dot_general | solution.py:43
  45.1 0.0 copy-start
  45.1 20.0 %gather_fusion.2 = bf16[768,5120]{1,0:T(8,128)(2,1)} fusion(bf16[1024,5120]{1,0:T(8,128)(2,1)} %fusion.3, s32[1024]{0:T(1024)S(1)} %pad_clamp_fusion), kind=kCustom, calls=%fused_computation.2 | custom fusion | bytes 15731712 | tf_op jit(solution)/shard_map/gather | solution.py:57
  65.1 0.0 copy-done
  65.1 3.2 %gather_fusion.1 = s32[768]{0:T(1024)S(1)} fusion(s32[1024]{0:T(1024)S(1)} %copy-done, s32[1024]{0:T(1024)S(1)} %pad_clamp_fusion), kind=kCustom, calls=%fused_computation.1 | custom fusion | bytes 9216 | tf_op jit(solution)/shard_map/gather | solution.py:64
  68.3 12.8 %fusion.32 = f32[1024,768]{0,1:T(8,128)S(1)} fusion(bf16[1024,5120]{1,0:T(8,128)(2,1)} %fusion.3, bf16[5120,768]{1,0:T(8,128)(2,1)} %param.15), kind=kOutput, calls=%fused_computation.67 | convolution fusion | flops 8053063680 | bytes 21495808 | tf_op jit(solution)/shard_map/dot_general | solution.py:40
  81.1 1.9 fusion.28
  83.0 2.1 copy.21
  85.1 3.3 %copy.20 = f32[1024,6,64]{2,0,1:T(8,128)} copy(f32[1024,6,64]{0,2,1:T(8,128)} %get-tuple-element.10) | data formatting | bytes 3145728
  88.4 11.0 %fusion.31 = f32[768,768]{0,1:T(8,128)S(1)} fusion(bf16[768,5120]{1,0:T(8,128)(2,1)} %gather_fusion.2, bf16[5120,768]{1,0:T(8,128)(2,1)} %param.14), kind=kOutput, calls=%fused_computation.66 | convolution fusion | flops 6039797760 | bytes 18087936 | tf_op jit(solution)/shard_map/dot_general | solution.py:57
  99.4 1.7 fusion.29
  101.1 2.9 %copy.19 = f32[768,6,64]{2,0,1:T(8,128)} copy(f32[768,6,64]{0,2,1:T(8,128)} %get-tuple-element.11) | data formatting | bytes 2359296
  104.0 3.2 %copy.18 = f32[768,6,64]{2,0,1:T(8,128)} copy(f32[768,6,64]{0,2,1:T(8,128)} %get-tuple-element.12) | data formatting | bytes 2359296
  107.2 1.9 multiply_cosine_fusion
  109.1 1.4 multiply_cosine_fusion.1
  110.6 1.7 fusion.9
  112.3 0.0 copy-start.2
  112.3 0.0 copy-start.3
  112.3 4.6 %subtract_convert_fusion = (bf16[1024,6,64]{2,0,1:T(8,128)(2,1)}, bf16[1024,6,64]{2,0,1:T(8,128)(2,1)}) fusion(f32[1024,6,64]{2,0,1:T(8,128)S(1)} %copy.21, f32[1024,6,64]{2,0,1:T(8,128)} %copy.20, f32[1024,64]{1,0:T(8,128)S(1)} %get-tuple-element.16, f32[1024,64]{1,0:T(8,128)S(1)} %get-tuple-element.15), kind=kLoop, calls=%fused_computation.21 | loop fusion | flops 3145728 | bytes 5242880 | tf_op jit(solution)/shard_map/convert
  116.9 0.0 copy-done.2
  116.9 0.0 copy-done.3
  116.9 0.0 copy-start.4
  116.9 0.0 copy-start.5
  116.9 2.0 subtract_convert_fusion.1
  118.9 0.0 copy-done.4
  118.9 0.5 copy-done.5
  119.4 13.2 %fusion.30 = (f32[6,768]{1,0:T(8,128)S(1)}, f32[6,768,1024]{2,1,0:T(8,128)}) fusion(pred[768,1024]{1,0:T(8,128)(4,1)} %fusion.9, bf16[1024,6,64]{2,0,1:T(8,128)(2,1)S(1)} %copy-done.5, bf16[1024,6,64]{2,0,1:T(8,128)(2,1)S(1)} %copy-done.4, bf16[768,6,64]{2,0,1:T(8,128)(2,1)} %get-tuple-element.8, bf16[768,6,64]{2,0,1:T(8,128)(2,1)} %get-tuple-element.7), kind=kOutput, calls=%fused_computation.65 | convolution fusion | flops 1232339968 | bytes 22431744 | tf_op jit(solution)/shard_map/sub | solution.py:69
  132.6 8.5 %fusion.12 = bf16[6,128,768]{2,1,0:T(8,128)(2,1)S(1)} fusion(bf16[1024,6,128]{0,2,1:T(8,128)(2,1)} %bitcast.41, f32[6,768,1024]{2,1,0:T(8,128)} %get-tuple-element.21, f32[6,768]{1,0:T(8,128)S(1)} %get-tuple-element.20), kind=kOutput, calls=%fused_computation.30 | convolution fusion | flops 1217986560 | bytes 21645312 | tf_op jit(solution)/shard_map/hqk,khd->qhd/dot_general | solution.py:71
  141.1 12.0 %select_convert_fusion = bf16[768,5120]{1,0:T(8,128)(2,1)} fusion(bf16[768,768]{0,1:T(8,128)(2,1)S(1)} %bitcast.42, bf16[768,5120]{1,0:T(8,128)(2,1)} %param.17, pred[768]{0:T(1024)(128)(4,1)S(1)} %broadcast_compare_fusion.1), kind=kOutput, calls=%fused_computation.13 | convolution fusion | flops 6047662080 | bytes 16909056 | tf_op jit(solution)/shard_map/dot_general | solution.py:73
  153.1 0.0 reduce-scatter.2.cloned.1.call-update
  153.1 20.0 %gather_fusion = bf16[768,5120]{1,0:T(8,128)(2,1)} fusion(bf16[1024,5120]{1,0:T(8,128)(2,1)} %param.9, s32[1024]{0:T(1024)S(1)} %pad_clamp_fusion), kind=kCustom, calls=%fused_computation | custom fusion | bytes 15731712 | tf_op jit(solution)/shard_map/gather | solution.py:75
  173.1 50.9 %reduce-scatter.2.cloned.1.call-done = bf16[768,1280]{1,0:T(8,128)(2,1)} async-done(((bf16[768,5120]{1,0:T(8,128)(2,1)}), bf16[768,1280]{1,0:T(8,128)(2,1)}) %reduce-scatter.2.cloned.1.call-update) | async-done | bytes 1966096 | tf_op jit(solution)/shard_map/reduce_scatter | solution.py:79
  224.0 2.8 add_convert_fusion
  226.8 50.9 %all_to_all.12 = bf16[8,96,1280]{2,1,0:T(8,128)(2,1)S(1)} all-to-all(bf16[8,96,1280]{2,1,0:T(8,128)(2,1)S(1)} %bitcast.35), channel_id=1, replica_groups=mesh['dp'=8,'mp'=4] {'dp'}, dimensions={0} | all-to-all | bytes 3932160 | tf_op jit(solution)/shard_map/all_to_all | solution.py:83
  277.7 1.3 copy.25
  (7 shorter events, 0.0 us)
Async XLA Ops:
  6.5 217.5 %reduce-scatter.2.cloned.1.call-start = ((), (), s32[]{:S(2)}) async-start(), calls=%async_computation.2 | async-start | bytes 9830400 | tf_op jit(solution)/shard_map/reduce_scatter | solution.py:79
  17.9 7.0 %copy-start.1 = (bf16[1024,5120]{1,0:T(8,128)(2,1)S(1)}, bf16[1024,5120]{1,0:T(8,128)(2,1)}, u32[]{:S(2)}) copy-start(bf16[1024,5120]{1,0:T(8,128)(2,1)} %param.9) | copy-start | bytes 31457284
  45.1 20.0 %copy-start = (s32[1024]{0:T(1024)S(1)}, s32[1024]{0:T(1024)}, u32[]{:S(2)}) copy-start(s32[1024]{0:T(1024)} %param.11) | copy-start | bytes 12292
  112.3 4.6 %copy-start.2 = (f32[768,6,64]{2,0,1:T(8,128)S(1)}, f32[768,6,64]{2,0,1:T(8,128)}, u32[]{:S(2)}) copy-start(f32[768,6,64]{2,0,1:T(8,128)} %copy.19) | copy-start | bytes 3538948
  112.3 4.6 %copy-start.3 = (f32[768,6,64]{2,0,1:T(8,128)S(1)}, f32[768,6,64]{2,0,1:T(8,128)}, u32[]{:S(2)}) copy-start(f32[768,6,64]{2,0,1:T(8,128)} %copy.18) | copy-start | bytes 3538948
  116.9 2.1 copy-start.4
  116.9 2.6 copy-start.5
Sparse Core Ops, SparseCore 0:
  153.3 70.6 reduce-scatter.1
where the time goes:
time: 290 us; the launch traced here: 286 us
  matrix products  71.6 us (25%)
  local copies, waits for them, and re-layouts  65.4 us (23%)
  waiting for transfers between devices  50.9 us (18%)
  blocking collectives  50.9 us (18%)
  other arithmetic  33.4 us (12%)
  between operations  13.7 us (5%)
    all_to_all x1, blocking collectives, body(): lax.all_to_all(updated, 'dp', split_axis=0, concat_axis=0, tiled=True)  50.9 us
    reduce_scatter x1, waiting for transfers between devices, body(): lax.psum_scatter(partial_value, 'mp', scatter_dimension=1, tiled=True)  50.9 us
    gather x1, local copies, waits for them, and re-layouts, body(): normed[picked]  20 us
    gather x1, local copies, waits for them, and re-layouts, body(): hidden[picked]  20 us
    dot_general x1, matrix products, body(): jnp.dot(normed, w_value, preferred_element_type=jnp.float32)  14.2 us
    unnamed x17, local copies, waits for them, and re-layouts  14 us
    sub x1, matrix products, body(): raised = jnp.exp(scores - highest)  13.2 us
    dot_general x1, matrix products, body(): jnp.dot(normed, w_key, preferred_element_type=jnp.float32)  12.8 us
  transfers between devices with their start and end apart: 1, of which 1 were waited for; matrix products, arithmetic and copies ran while one was open for 7% of the time, Pallas kernels for 0%

commit v1 on v0

v1 whole, which is shorter than its diff:
```python
import functools
import math

import jax
import jax.numpy as jnp
import numpy as np
from jax import lax
from jax.experimental import pallas as pl
from jax.experimental.pallas import tpu as pltpu
from jax.sharding import PartitionSpec as P

HD = 128
ANY = pl.ANY
VMEM = pltpu.VMEM


def rope_tables(tokens):
    half = HD // 2
    frequency = 10000.0 ** (-np.arange(half, dtype=np.float64) / half)
    angle = np.arange(tokens, dtype=np.float64)[:, None] * frequency[None, :]
    cosine, sine = np.cos(angle), np.sin(angle)
    return (
        np.concatenate([cosine, cosine], axis=1).astype(np.float32),
        np.concatenate([-sine, sine], axis=1).astype(np.float32),
    )


def qkv_kernel(
    blocks, bn, rows, hidden, gain, wq, wk, wv, cosine, sine, out, held, normed, wbuf, hsem, wsem
):
    step = pl.program_id(0)
    slot = lax.rem(step, 2)
    chunks = hidden.shape[0] // rows

    def fetch(index, do):
        for which, w in enumerate((wq, wk, wv)):

            @pl.when(index // blocks == which)
            def _():
                column = pl.multiple_of(lax.rem(index, blocks) * bn, bn)
                to = lax.rem(index, 2)
                do(pltpu.make_async_copy(w.at[:, pl.ds(column, bn)], wbuf.at[to], wsem.at[to]))

    def hidden_copy(r):
        part = pl.ds(r * rows, rows)
        return pltpu.make_async_copy(hidden.at[part], held.at[part], hsem.at[r])

    @pl.when(step == 0)
    def _():
        for r in range(chunks):
            hidden_copy(r).start()
        fetch(0, lambda c: c.start())

    @pl.when(step + 1 < 3 * blocks)
    def _():
        fetch(step + 1, lambda c: c.start())

    @pl.when(step == 0)
    def _():
        def normalize(r, carry):
            hidden_copy(r).wait()
            part = pl.ds(pl.multiple_of(r * rows, rows), rows)
            x = held[part, :].astype(jnp.float32)
            mean_square = jnp.mean(x * x, axis=-1, keepdims=True)
            y = x * lax.rsqrt(mean_square + 1e-05) * gain[...].astype(jnp.float32)
            normed[part, :] = y.astype(jnp.bfloat16)
            return carry

        lax.fori_loop(0, chunks, normalize, 0)

    fetch(step, lambda c: c.wait())
    big = 2 * rows

    def product(r, rotate):
        part = pl.ds(pl.multiple_of(r * big, big), big)
        y = jnp.dot(normed[part, :], wbuf[slot], preferred_element_type=jnp.float32)
        for h in range(bn // HD):
            lanes = slice(h * HD, (h + 1) * HD)
            z = y[:, lanes]
            if rotate:
                z = z * cosine[part, :] + pltpu.roll(z, HD // 2, 1) * sine[part, :]
            out[0, part, lanes] = z.astype(jnp.bfloat16)

    for rotate in (True, False):

        @pl.when((step < 2 * blocks) == rotate)
        def _():
            def go(r, carry):
                product(r, rotate)
                return carry

            lax.fori_loop(0, hidden.shape[0] // big, go, 0)


def project(hidden, gain, wq, wk, wv):
    tokens, width = hidden.shape
    hw = wq.shape[1]
    bn = 256 if hw % 256 == 0 else HD
    blocks = hw // bn
    rows = 128
    cosine, sine = rope_tables(tokens)
    whole = lambda *shape: pl.BlockSpec(shape, lambda i: (0,) * len(shape), pipeline_mode=pl.Buffered(1))
    return pl.pallas_call(
        functools.partial(qkv_kernel, blocks, bn, rows),
        grid=(3 * blocks,),
        out_shape=jax.ShapeDtypeStruct((3, tokens, hw), jnp.bfloat16),
        in_specs=[
            pl.BlockSpec(memory_space=ANY),
            whole(1, width),
            pl.BlockSpec(memory_space=ANY),
            pl.BlockSpec(memory_space=ANY),
            pl.BlockSpec(memory_space=ANY),
            whole(tokens, HD),
            whole(tokens, HD),
        ],
        out_specs=pl.BlockSpec((1, tokens, bn), lambda i: (i // blocks, 0, lax.rem(i, blocks))),
        scratch_shapes=[
            VMEM((tokens, width), jnp.bfloat16),
            VMEM((tokens, width), jnp.bfloat16),
            VMEM((2, width, bn), jnp.bfloat16),
            pltpu.SemaphoreType.DMA((tokens // rows,)),
            pltpu.SemaphoreType.DMA((2,)),
        ],
        compiler_params=pltpu.CompilerParams(vmem_limit_bytes=60 * 2**20),
        name="qkv",
    )(hidden, gain.reshape(1, width), wq, wk, wv, cosine, sine)


def attention_kernel(capacity, q, k, v, meta_row, meta_col, out, pick, bias, attended):
    tokens = q.shape[1]
    slots = out.shape[0]
    block = 256
    scale = 1.0 / math.sqrt(HD)

    @pl.when(pl.program_id(0) == 0)
    def _():
        code = meta_row[1:2, :]
        rank = jnp.zeros((1, tokens), jnp.float32)
        for b in range(tokens // block):
            part = slice(b * block, (b + 1) * block)
            below = lax.broadcasted_iota(jnp.int32, (block, tokens), 0) + b * block
            across = lax.broadcasted_iota(jnp.int32, (block, tokens), 1)
            earlier = (meta_col[part, 1:2] == code) & (below < across)
            rank += jnp.sum(jnp.where(earlier, 1.0, 0.0), axis=0, keepdims=True)
            allowed = (meta_col[part, 0:1] == meta_row[0:1, :]) & (across <= below)
            bias[part, :] = jnp.where(allowed, 0.0, -1e30)
        slot = jnp.where(code >= 0, code * capacity + rank.astype(jnp.int32), -1)
        for s in range(0, slots, 128):
            row = lax.broadcasted_iota(jnp.int32, (128, tokens), 0) + s
            pick[s : s + 128, :] = jnp.where(row == slot, 1.0, 0.0).astype(jnp.bfloat16)

    for b in range(tokens // block):
        part = slice(b * block, (b + 1) * block)
        end = (b + 1) * block
        scores = lax.dot_general(
            q[0, part, :], k[0, :end, :], (((1,), (1,)), ((), ())), preferred_element_type=jnp.float32
        )
        scores = scores * scale + bias[part, :end]
        raised = jnp.exp(scores - jnp.max(scores, axis=-1, keepdims=True))
        total = jnp.sum(raised, axis=-1, keepdims=True)
        mixed = jnp.dot(raised.astype(jnp.bfloat16), v[0, :end, :], preferred_element_type=jnp.float32)
        attended[part, :] = (mixed / total).astype(jnp.bfloat16)
    out[...] = jnp.dot(pick[...], attended[...], preferred_element_type=jnp.float32).astype(jnp.bfloat16)


def attend(qkv, meta, slots, capacity):
    _, tokens, hw = qkv.shape
    part = lambda which: pl.BlockSpec((1, tokens, HD), lambda h: (which, 0, h))
    return pl.pallas_call(
        functools.partial(attention_kernel, capacity),
        grid=(hw // HD,),
        out_shape=(
            jax.ShapeDtypeStruct((slots, hw), jnp.bfloat16),
            jax.ShapeDtypeStruct((slots, tokens), jnp.bfloat16),
        ),
        in_specs=[
            part(0),
            part(1),
            part(2),
            pl.BlockSpec((2, tokens), lambda h: (0, 0)),
            pl.BlockSpec((tokens, 2), lambda h: (0, 0)),
        ],
        out_specs=(
            pl.BlockSpec((slots, HD), lambda h: (0, h)),
            pl.BlockSpec((slots, tokens), lambda h: (0, 0)),
        ),
        scratch_shapes=[VMEM((tokens, tokens), jnp.float32), VMEM((tokens, HD), jnp.bfloat16)],
        compiler_params=pltpu.CompilerParams(vmem_limit_bytes=48 * 2**20),
        name="attend",
    )(qkv, qkv, qkv, meta, meta.T)


def body(hidden, exit_depth, seq_ids, dest, norm_gain, w_query, w_key, w_value, w_out):
    peers = lax.axis_size("dp")
    groups = lax.axis_size("mp")
    tokens, width = hidden.shape
    slots = 3 * tokens // 4
    capacity = slots // peers
    feature_slice = width // groups
    meta = jnp.stack([seq_ids, jnp.where(exit_depth == 3, dest, -1)])
    qkv = project(hidden, norm_gain, w_query, w_key, w_value)
    attended, pick = attend(qkv, meta, slots, capacity)
    own_hidden = lax.dynamic_slice_in_dim(
        hidden, lax.axis_index("mp") * feature_slice, feature_slice, 1
    )
    partial_value = jnp.dot(attended, w_out, preferred_element_type=jnp.float32).astype(jnp.bfloat16)
    own_features = jnp.dot(pick, own_hidden, preferred_element_type=jnp.float32)
    summed = lax.psum_scatter(partial_value, "mp", scatter_dimension=1, tiled=True).astype(
        jnp.float32
    )
    updated = (own_features + summed).astype(jnp.bfloat16)
    return lax.all_to_all(updated, "dp", split_axis=0, concat_axis=0, tiled=True)


def solution(mesh):
    return jax.shard_map(
        body,
        mesh=mesh,
        in_specs=(
            P("dp", None),
            P("dp"),
            P("dp"),
            P("dp"),
            P(),
            P(None, "mp"),
            P(None, "mp"),
            P(None, "mp"),
            P("mp", None),
        ),
        out_specs=P("dp", "mp"),
        check_vma=False,
    )
```

time: 290 us -> 211 us (0.73); the launches traced: 286 us -> 210 us
  local copies, waits for them, and re-layouts: 65.4 us -> 2.82 us
  matrix products: 71.6 us -> 13 us
  Pallas kernels: 0 us -> 58 us
  other arithmetic: 33.4 us -> 1.4 us
  waiting for transfers between devices: 50.9 us -> 70.9 us
    pallas_call x0 -> x2, Pallas kernels: none -> 58 us  [the longest x1 42.4 us: project(): pl.pallas_call(functools.partial(qkv_kernel, blocks, bn, rows), grid=(3 *...]
    dot_general x5 -> x2, matrix products: 58.5 us -> 13 us  [the longest x1 8.45 us: body(): jnp.dot(attended, w_out, preferred_element_type=jnp.float32)]
    gather x3 -> x0, local copies, waits for them, and re-layouts: 43.2 us -> none  [the longest x1 20 us: body(): normed[picked]]
    reduce_scatter x1, waiting for transfers between devices: 50.9 us -> 70.8 us  [body(): lax.psum_scatter(partial_value, 'mp', scatter_dimension=1, tiled=True)]
    sub x1 -> x0, matrix products: 13.2 us -> none  [body(): raised = jnp.exp(scores - highest)]
    unnamed x17 -> x3, local copies, waits for them, and re-layouts: 14 us -> 1.28 us
    convert_element_type x6 -> x0, other arithmetic: 10.3 us -> none  [the longest x1 6.05 us: body(): (widened * lax.rsqrt(mean_square + 1e-05) * norm_gain.astype(jnp.float32)...]
    another operation x4 -> x1, other arithmetic: 9.05 us -> 0.7 us  [body(): meta = jnp.stack([seq_ids, jnp.where(exit_depth == 3, dest, -1)])]
  transfers between devices with their start and end apart: 1 -> 1, of which waited for: 1 -> 1; matrix products, arithmetic and copies ran while one was open for 7% -> 0% of each run, Pallas kernels for 0% -> 0%
where the time goes in v1:
time: 211 us; the launch traced here: 210 us
  waiting for transfers between devices  70.9 us (34%)
  Pallas kernels  58 us (27%)
  blocking collectives  50.9 us (24%)
  between operations  13.4 us (6%)
  matrix products  13 us (6%)
  local copies, waits for them, and re-layouts  2.82 us (1%)
    reduce_scatter x1, waiting for transfers between devices, body(): lax.psum_scatter(partial_value, 'mp', scatter_dimension=1, tiled=True)  70.8 us
    all_to_all x1, blocking collectives, body(): lax.all_to_all(updated, 'dp', split_axis=0, concat_axis=0, tiled=True)  50.9 us
    pallas_call x1, Pallas kernels, project(): pl.pallas_call(functools.partial(qkv_kernel, blocks, bn, rows), grid=(3 *...  42.4 us
    pallas_call x1, Pallas kernels, attend(): pl.pallas_call(functools.partial(attention_kernel, capacity), grid=(hw //...  15.6 us
    dot_general x1, matrix products, body(): jnp.dot(attended, w_out, preferred_element_type=jnp.float32)  8.45 us
    dot_general x1, matrix products, body(): own_features = jnp.dot(pick, own_hidden, preferred_element_type=jnp.float32)  4.54 us
  transfers between devices with their start and end apart: 1, of which 1 were waited for; matrix products, arithmetic and copies ran while one was open for 0% of the time, Pallas kernels for 0%

profile of v1, /device:TPU:0, one launch (start us, length us, event | category | flops | bytes accessed | tf_op | source)
XLA Modules:
  0.0 210.5 jit_solution(8419207803696782744)
XLA Ops:
  6.5 0.0 reduce-scatter.2.cloned.1.call-start
  6.5 1.3 reshape.5.gain
  7.9 0.7 compare_select_fusion
  8.6 0.7 pad_add_fusion.meta_row
  9.3 0.2 copy.16
  9.5 42.4 %qkv.1.q.k.v = bf16[3,1024,768]{2,1,0:T(8,128)(2,1)} custom-call(bf16[1024,5120]{1,0:T(8,128)(2,1)} %hidden.1, bf16[1,5120]{1,0:T(2,128)(2,1)} %reshape.5.gain, bf16[5120,768]{1,0:T(8,128)(2,1)} %wq.1, bf16[5120,768]{1,0:T(8,128)(2,1)} %wk.1, bf16[5120,768]{1,0:T(8,128)(2,1)} %wv.1, f32[1024,128]{1,0:T(8,128)} %constant.18.clone.cosine, ...), custom_call_target="tpu_custom_call" | custom-call | tf_op jit(solution)/shard_map/qkv/pallas_call | solution.py:103
  51.9 0.0 copy-start
  51.9 15.6 %attend.1 = (bf16[768,768]{1,0:T(8,128)(2,1)S(1)}, bf16[768,1024]{1,0:T(8,128)(2,1)S(1)}) custom-call(bf16[3,1024,768]{2,1,0:T(8,128)(2,1)} %qkv.1.q.k.v, bf16[3,1024,768]{2,1,0:T(8,128)(2,1)} %qkv.1.q.k.v, bf16[3,1024,768]{2,1,0:T(8,128)(2,1)} %qkv.1.q.k.v, s32[2,1024]{1,0:T(2,128)S(1)} %pad_add_fusion.meta_row, s32[1024,2]{1,0:T(8,128)S(1)} %bitcast.8), custom_call_target="tpu_custom_call" | custom-call | tf_op jit(solution)/shard_map/attend/pallas_call | solution.py:169
  67.5 0.0 copy-done
  67.6 8.5 %convolution_convert_fusion = bf16[768,5120]{1,0:T(8,128)(2,1)} fusion(bf16[768,768]{1,0:T(8,128)(2,1)S(1)} %get-tuple-element.8, bf16[768,5120]{1,0:T(8,128)(2,1)S(1)} %copy-done), kind=kOutput, calls=%fused_computation | convolution fusion | flops 6043729920 | bytes 16908288 | tf_op jit(solution)/shard_map/dot_general | solution.py:206
  76.0 0.0 reduce-scatter.2.cloned.1.call-update
  76.0 70.8 %reduce-scatter.2.cloned.1.call-done = bf16[768,1280]{1,0:T(8,128)(2,1)} async-done(((bf16[768,5120]{1,0:T(8,128)(2,1)}), bf16[768,1280]{1,0:T(8,128)(2,1)}) %reduce-scatter.2.cloned.1.call-update) | async-done | bytes 1966096 | tf_op jit(solution)/shard_map/reduce_scatter | solution.py:208
  146.9 4.5 %add_convert_fusion = bf16[768,1280]{1,0:T(8,128)(2,1)S(1)} fusion(bf16[768,1280]{1,0:T(8,128)(2,1)} %reduce-scatter.2.cloned.1.call-done, bf16[768,1024]{1,0:T(8,128)(2,1)S(1)} %get-tuple-element.7, bf16[1024,5120]{1,0:T(8,128)(2,1)} %hidden.1, s32[]{:T(128)S(6)} %select_n.8), kind=kOutput, calls=%fused_computation.1 | convolution fusion | flops 2016215040 | bytes 8126468 | tf_op jit(solution)/shard_map/dot_general | solution.py:207
  151.4 50.9 %all_to_all.12 = bf16[8,96,1280]{2,1,0:T(8,128)(2,1)S(1)} all-to-all(bf16[8,96,1280]{2,1,0:T(8,128)(2,1)S(1)} %bitcast.10), channel_id=1, replica_groups=mesh['dp'=8,'mp'=4] {'dp'}, dimensions={0} | all-to-all | bytes 3932160 | tf_op jit(solution)/shard_map/all_to_all | solution.py:212
  202.4 1.3 copy.18
Async XLA Ops:
  6.5 140.3 %reduce-scatter.2.cloned.1.call-start = ((), (), s32[]{:S(2)}) async-start(), calls=%async_computation.2 | async-start | bytes 9830400 | tf_op jit(solution)/shard_map/reduce_scatter | solution.py:208
  51.9 15.6 %copy-start = (bf16[768,5120]{1,0:T(8,128)(2,1)S(1)}, bf16[768,5120]{1,0:T(8,128)(2,1)}, u32[]{:S(2)}) copy-start(bf16[768,5120]{1,0:T(8,128)(2,1)} %param.19) | copy-start | bytes 23592964
Sparse Core Ops, SparseCore 0:
  76.2 70.6 reduce-scatter.1

commit v2 on v1

--- a/solution.py
+++ b/solution.py
@@ -10,6 +10,7 @@
 from jax.sharding import PartitionSpec as P
 
 HD = 128
+CHUNK = 256
 ANY = pl.ANY
 VMEM = pltpu.VMEM
 
@@ -190,26 +191,191 @@
     )(qkv, qkv, qkv, meta, meta.T)
 
 
+def out_kernel(
+    peers, groups, att, pick, hidden, w_out, out,
+    wbuf, residual, pair_send, pair_own, pair_recv, x_send, x_recv, acc, updated,
+    wsem, rsem, pair_ssem, pair_rsem, x_ssem, x_rsem, row_ssem, row_rsem, own_sem,
+):
+    chunks, _, slots, cw = pair_send.shape
+    capacity = slots // peers
+    inner = w_out.shape[0]
+    feature_slice = w_out.shape[1] // groups
+    ring = groups // 2
+    d, m = lax.axis_index("dp"), lax.axis_index("mp")
+    core, x = lax.rem(m, 2), m // 2
+    partner = x * 2 + 1 - core
+
+    def x_to(r):
+        return lax.rem(x + r, ring)
+
+    def lane(n, j):
+        return pl.ds(pl.multiple_of(n * feature_slice + j * cw, HD), cw)
+
+    def weight_copy(j, n):
+        return pltpu.make_async_copy(w_out.at[:, lane(n, j)], wbuf.at[j, n], wsem.at[j, n])
+
+    def residual_copy(j):
+        return pltpu.make_async_copy(hidden.at[:, lane(m, j)], residual.at[j], rsem.at[j])
+
+    def pair_copy(j):
+        return pltpu.make_async_remote_copy(
+            src_ref=pair_send.at[j], dst_ref=pair_recv.at[j],
+            send_sem=pair_ssem.at[j], recv_sem=pair_rsem.at[j],
+            device_id={"mp": partner}, device_id_type=pl.DeviceIdType.MESH,
+        )
+
+    def x_copy(j, r):
+        return pltpu.make_async_remote_copy(
+            src_ref=x_send.at[j, r - 1], dst_ref=x_recv.at[j, r - 1],
+            send_sem=x_ssem.at[j, r - 1], recv_sem=x_rsem.at[j, r - 1],
+            device_id={"mp": x_to(r) * 2 + core}, device_id_type=pl.DeviceIdType.MESH,
+        )
+
+    def rows_of(t):
+        return pl.ds(pl.multiple_of(t * capacity, 16), capacity)
+
+    def own_rows(j):
+        return out.at[rows_of(d), pl.ds(pl.multiple_of(j * cw, HD), cw)]
+
+    def row_copy(j, i):
+        to = lax.rem(d + i, peers)
+        return pltpu.make_async_remote_copy(
+            src_ref=updated.at[j, rows_of(to)], dst_ref=own_rows(j),
+            send_sem=row_ssem.at[j, i], recv_sem=row_rsem.at[j, i],
+            device_id={"dp": to}, device_id_type=pl.DeviceIdType.MESH,
+        )
+
+    def own_copy(j):
+        return pltpu.make_async_copy(updated.at[j, rows_of(d)], own_rows(j), own_sem.at[j])
+
+    for j in range(chunks):
+        for n in range(groups):
+            weight_copy(j, n).start()
+        residual_copy(j).start()
+
+    barrier = pltpu.get_barrier_semaphore()
+    for i in range(1, peers):
+        pl.semaphore_signal(
+            barrier, inc=1, device_id={"dp": lax.rem(d + i, peers)}, device_id_type=pl.DeviceIdType.MESH
+        )
+    for r in range(1, ring):
+        pl.semaphore_signal(
+            barrier, inc=1, device_id={"mp": x_to(r) * 2 + core}, device_id_type=pl.DeviceIdType.MESH
+        )
+    pl.semaphore_signal(
+        barrier, inc=1, device_id={"mp": partner}, device_id_type=pl.DeviceIdType.MESH
+    )
+    pl.semaphore_wait(barrier, peers + ring - 1)
+
+    def multiply(j, n):
+        return jnp.dot(att[...], wbuf[j, n], preferred_element_type=jnp.float32).astype(jnp.bfloat16)
+
+    def step(s, carry):
+        @pl.when(s < chunks)
+        def _():
+            for n in range(groups):
+                weight_copy(s, n).wait()
+            for r in range(ring):
+                pair_send[s, r] = multiply(s, x_to(r) * 2 + 1 - core)
+            pair_copy(s).start()
+            for r in range(ring):
+                pair_own[s, r] = multiply(s, x_to(r) * 2 + core)
+
+        @pl.when((s >= 1) & (s <= chunks))
+        def _():
+            j = s - 1
+            pair_copy(j).wait_recv()
+            for r in range(1, ring):
+                total = pair_own[j, r].astype(jnp.float32) + pair_recv[j, r].astype(jnp.float32)
+                x_send[j, r - 1] = total.astype(jnp.bfloat16)
+                x_copy(j, r).start()
+            residual_copy(j).wait()
+            kept = jnp.dot(pick[...], residual[j], preferred_element_type=jnp.float32)
+            acc[j] = (
+                kept + pair_own[j, 0].astype(jnp.float32) + pair_recv[j, 0].astype(jnp.float32)
+            )
+
+        @pl.when(s >= 2)
+        def _():
+            j = s - 2
+            total = acc[j]
+            for r in range(1, ring):
+                x_copy(j, r).wait_recv()
+                total += x_recv[j, r - 1].astype(jnp.float32)
+            updated[j] = total.astype(jnp.bfloat16)
+            for i in range(1, peers):
+                row_copy(j, i).start()
+            own_copy(j).start()
+
+        return carry
+
+    lax.fori_loop(0, chunks + 2, step, 0)
+
+    def drain(j, carry):
+        pair_copy(j).wait_send()
+        for r in range(1, ring):
+            x_copy(j, r).wait_send()
+        own_copy(j).wait()
+        for i in range(1, peers):
+            row_copy(j, i).wait()
+        return carry
+
+    lax.fori_loop(0, chunks, drain, 0)
+
+
+def finish(attended, pick, hidden, w_out, peers, groups):
+    slots, inner = attended.shape
+    tokens, width = hidden.shape
+    feature_slice = width // groups
+    cw = CHUNK if feature_slice % CHUNK == 0 else HD
+    chunks = feature_slice // cw
+    ring = groups // 2
+    dma = pltpu.SemaphoreType.DMA
+    bf16 = jnp.bfloat16
+    vmem = pl.BlockSpec(memory_space=VMEM)
+    far = pl.BlockSpec(memory_space=ANY)
+    return pl.pallas_call(
+        functools.partial(out_kernel, peers, groups),
+        out_shape=jax.ShapeDtypeStruct((slots, feature_slice), bf16),
+        in_specs=[vmem, vmem, far, far],
+        out_specs=far,
+        scratch_shapes=[
+            VMEM((chunks, groups, inner, cw), bf16),
+            VMEM((chunks, tokens, cw), bf16),
+            VMEM((chunks, ring, slots, cw), bf16),
+            VMEM((chunks, ring, slots, cw), bf16),
+            VMEM((chunks, ring, slots, cw), bf16),
+            VMEM((chunks, ring - 1, slots, cw), bf16),
+            VMEM((chunks, ring - 1, slots, cw), bf16),
+            VMEM((chunks, slots, cw), jnp.float32),
+            VMEM((chunks, slots, cw), bf16),
+            dma((chunks, groups)),
+            dma((chunks,)),
+            dma((chunks,)),
+            dma((chunks,)),
+            dma((chunks, ring - 1)),
+            dma((chunks, ring - 1)),
+            dma((chunks, peers)),
+            dma((chunks, peers)),
+            dma((chunks,)),
+        ],
+        compiler_params=pltpu.CompilerParams(
+            collective_id=0, has_side_effects=True, vmem_limit_bytes=60 * 2**20
+        ),
+        name="finish",
+    )(attended, pick, hidden, w_out)
+
+
 def body(hidden, exit_depth, seq_ids, dest, norm_gain, w_query, w_key, w_value, w_out):
     peers = lax.axis_size("dp")
     groups = lax.axis_size("mp")
-    tokens, width = hidden.shape
+    tokens = hidden.shape[0]
     slots = 3 * tokens // 4
     capacity = slots // peers
-    feature_slice = width // groups
     meta = jnp.stack([seq_ids, jnp.where(exit_depth == 3, dest, -1)])
     qkv = project(hidden, norm_gain, w_query, w_key, w_value)
     attended, pick = attend(qkv, meta, slots, capacity)
-    own_hidden = lax.dynamic_slice_in_dim(
-        hidden, lax.axis_index("mp") * feature_slice, feature_slice, 1
-    )
-    partial_value = jnp.dot(attended, w_out, preferred_element_type=jnp.float32).astype(jnp.bfloat16)
-    own_features = jnp.dot(pick, own_hidden, preferred_element_type=jnp.float32)
-    summed = lax.psum_scatter(partial_value, "mp", scatter_dimension=1, tiled=True).astype(
-        jnp.float32
-    )
-    updated = (own_features + summed).astype(jnp.bfloat16)
-    return lax.all_to_all(updated, "dp", split_axis=0, concat_axis=0, tiled=True)
+    return finish(attended, pick, hidden, w_out, peers, groups)
 
 
 def solution(mesh):

time: 211 us -> 130 us (0.62)
  waiting for transfers between devices: 70.9 us -> 0 us
  Pallas kernels: 58 us -> 122 us
  blocking collectives: 50.9 us -> 0 us
  between operations: 13.4 us -> 0.05 us
  matrix products: 13 us -> 0 us
  local copies, waits for them, and re-layouts: 2.82 us -> 6.67 us
    reduce_scatter x1 -> x0, waiting for transfers between devices: 70.8 us -> none  [body(): lax.psum_scatter(partial_value, 'mp', scatter_dimension=1, tiled=True)]
    pallas_call x0 -> x1, Pallas kernels: none -> 63.8 us  [finish(): pl.pallas_call(functools.partial(out_kernel, peers, groups), out_shape=ja...]
    all_to_all x1 -> x0, blocking collectives: 50.9 us -> none  [body(): lax.all_to_all(updated, 'dp', split_axis=0, concat_axis=0, tiled=True)]
    dot_general x2 -> x0, matrix products: 13 us -> none  [the longest x1 8.45 us: body(): jnp.dot(attended, w_out, preferred_element_type=jnp.float32)]
    unnamed x3 -> x5, local copies, waits for them, and re-layouts: 1.28 us -> 5.12 us
  transfers between devices with their start and end apart: 1 -> 0, of which waited for: 1 -> 0; matrix products, arithmetic and copies ran while one was open for 0% -> 0% of each run, Pallas kernels for 0% -> 0%
where the time goes in v2:
time: 130 us
  Pallas kernels  122 us (94%)
  local copies, waits for them, and re-layouts  6.67 us (5%)
  other arithmetic  1.4 us (1%)
    pallas_call x1, Pallas kernels, finish(): pl.pallas_call(functools.partial(out_kernel, peers, groups), out_shape=ja...  63.8 us
    pallas_call x1, Pallas kernels, project(): pl.pallas_call(functools.partial(qkv_kernel, blocks, bn, rows), grid=(3 *...  42.4 us
    pallas_call x1, Pallas kernels, attend(): pl.pallas_call(functools.partial(attention_kernel, capacity), grid=(hw //...  15.4 us
    unnamed x5, local copies, waits for them, and re-layouts  5.12 us

profile of v2, /device:TPU:0, one launch (start us, length us, event | category | flops | bytes accessed | tf_op | source)
XLA Modules:
  0.0 129.7 jit_solution(9974811182451235009)
XLA Ops:
  0.0 0.7 compare_select_fusion
  0.7 0.7 pad_add_fusion.meta_row
  1.4 1.3 %reshape.3.gain = bf16[1,5120]{1,0:T(2,128)(2,1)} reshape(bf16[5120]{0:T(1024)(128)(2,1)} %param.15) | data formatting | bytes 20480 | tf_op jit(solution)/shard_map/reshape | solution.py:127
  2.7 0.2 copy.16
  3.0 42.4 %qkv.1.q.k.v = bf16[3,1024,768]{2,1,0:T(8,128)(2,1)} custom-call(bf16[1024,5120]{1,0:T(8,128)(2,1)} %hidden.3, bf16[1,5120]{1,0:T(2,128)(2,1)} %reshape.3.gain, bf16[5120,768]{1,0:T(8,128)(2,1)} %wq.1, bf16[5120,768]{1,0:T(8,128)(2,1)} %wk.1, bf16[5120,768]{1,0:T(8,128)(2,1)} %wv.1, f32[1024,128]{1,0:T(8,128)} %constant.8.clone.cosine, ...), custom_call_target="tpu_custom_call" | custom-call | tf_op jit(solution)/shard_map/qkv/pallas_call | solution.py:104
  45.4 15.4 %attend.1 = (bf16[768,768]{1,0:T(8,128)(2,1)S(1)}, bf16[768,1024]{1,0:T(8,128)(2,1)S(1)}) custom-call(bf16[3,1024,768]{2,1,0:T(8,128)(2,1)} %qkv.1.q.k.v, bf16[3,1024,768]{2,1,0:T(8,128)(2,1)} %qkv.1.q.k.v, bf16[3,1024,768]{2,1,0:T(8,128)(2,1)} %qkv.1.q.k.v, s32[2,1024]{1,0:T(2,128)S(1)} %pad_add_fusion.meta_row, s32[1024,2]{1,0:T(8,128)S(1)} %bitcast.3), custom_call_target="tpu_custom_call" | custom-call | tf_op jit(solution)/shard_map/attend/pallas_call | solution.py:170
  60.8 0.0 copy-start
  60.9 1.1 copy-done
  62.0 0.0 copy-start.1
  62.0 1.0 copy-done.1
  63.0 63.8 %finish.1 = bf16[768,1280]{1,0:T(8,128)(2,1)} custom-call(bf16[768,768]{1,0:T(8,128)(2,1)} %copy-done.1, bf16[768,1024]{1,0:T(8,128)(2,1)} %copy-done, bf16[1024,5120]{1,0:T(8,128)(2,1)} %hidden.3, bf16[768,5120]{1,0:T(8,128)(2,1)} %w_out.1), custom_call_target="tpu_custom_call" | custom-call | tf_op jit(solution)/shard_map/finish/pallas_call | solution.py:337
  126.8 2.9 %copy.18 = bf16[768,1280]{1,0:T(8,128)(2,1)} copy(bf16[768,1280]{1,0:T(8,128)(2,1)} %finish.1) | data formatting | bytes 3932160
Async XLA Ops:
  60.8 1.1 copy-start
  62.0 1.0 copy-start.1

commit v3 on v1

--- a/solution.py
+++ b/solution.py
@@ -10,6 +10,8 @@
 from jax.sharding import PartitionSpec as P
 
 HD = 128
+CHUNKS = 8
+LAG = 1
 ANY = pl.ANY
 VMEM = pltpu.VMEM
 
@@ -126,90 +128,243 @@
     )(hidden, gain.reshape(1, width), wq, wk, wv, cosine, sine)
 
 
-def attention_kernel(capacity, q, k, v, meta_row, meta_col, out, pick, bias, attended):
-    tokens = q.shape[1]
-    slots = out.shape[0]
+def tail_kernel(
+    peers, groups, per_chunk, qkv, meta_row, meta_col, hidden, w_out, out,
+    wbuf, residual, slot_row, pair_send, pair_own, pair_recv, x_send, x_recv, acc, updated,
+    wsem, rsem, pair_ssem, pair_rsem, x_ssem, x_rsem, row_ssem, row_rsem, own_sem,
+):
+    chunks, ring, rows, feature_slice = pair_send.shape
+    capacity = rows // per_chunk
+    _, tokens, inner = qkv.shape
+    d, m = lax.axis_index("dp"), lax.axis_index("mp")
+    core, x = lax.rem(m, 2), m // 2
+    partner = x * 2 + 1 - core
+    scale = 1.0 / math.sqrt(HD)
+    mesh_id = pl.DeviceIdType.MESH
+
+    def x_to(r):
+        return lax.rem(x + r, ring)
+
+    def target(i):
+        away = peers // 2 + ((i + 1) // 2) * (1 - 2 * lax.rem(i, 2))
+        return lax.rem(d + away, peers)
+
+    def weight_copy(n):
+        columns = pl.ds(n * feature_slice, feature_slice)
+        return pltpu.make_async_copy(w_out.at[:, columns], wbuf.at[n], wsem.at[n])
+
+    def residual_copy():
+        columns = pl.ds(pl.multiple_of(m * feature_slice, HD), feature_slice)
+        return pltpu.make_async_copy(hidden.at[:, columns], residual, rsem)
+
+    def pair_copy(j):
+        return pltpu.make_async_remote_copy(
+            src_ref=pair_send.at[j], dst_ref=pair_recv.at[j],
+            send_sem=pair_ssem.at[j], recv_sem=pair_rsem.at[j],
+            device_id={"mp": partner}, device_id_type=mesh_id,
+        )
+
+    def x_copy(j, r):
+        return pltpu.make_async_remote_copy(
+            src_ref=x_send.at[j, r - 1], dst_ref=x_recv.at[j, r - 1],
+            send_sem=x_ssem.at[j, r - 1], recv_sem=x_rsem.at[j, r - 1],
+            device_id={"mp": x_to(r) * 2 + core}, device_id_type=mesh_id,
+        )
+
+    def own_rows():
+        return out.at[pl.ds(pl.multiple_of(d * capacity, 16), capacity)]
+
+    def row_copy(j, k):
+        return pltpu.make_async_remote_copy(
+            src_ref=updated.at[j, pl.ds(k * capacity, capacity)], dst_ref=own_rows(),
+            send_sem=row_ssem.at[j, k], recv_sem=row_rsem.at[j, k],
+            device_id={"dp": target(j * per_chunk + k)}, device_id_type=mesh_id,
+        )
+
+    def own_copy():
+        return pltpu.make_async_copy(
+            updated.at[chunks - 1, pl.ds(rows - capacity, capacity)], own_rows(), own_sem
+        )
+
+    for n in range(groups):
+        weight_copy(n).start()
+    residual_copy().start()
+
+    barrier = pltpu.get_barrier_semaphore()
+    for i in range(1, peers):
+        pl.semaphore_signal(
+            barrier, inc=1, device_id={"dp": lax.rem(d + i, peers)}, device_id_type=mesh_id
+        )
+    for r in range(1, ring):
+        pl.semaphore_signal(
+            barrier, inc=1, device_id={"mp": x_to(r) * 2 + core}, device_id_type=mesh_id
+        )
+    pl.semaphore_signal(barrier, inc=1, device_id={"mp": partner}, device_id_type=mesh_id)
+
+    code = meta_row[1:2, :]
     block = 256
-    scale = 1.0 / math.sqrt(HD)
-
-    @pl.when(pl.program_id(0) == 0)
-    def _():
-        code = meta_row[1:2, :]
-        rank = jnp.zeros((1, tokens), jnp.float32)
-        for b in range(tokens // block):
-            part = slice(b * block, (b + 1) * block)
-            below = lax.broadcasted_iota(jnp.int32, (block, tokens), 0) + b * block
-            across = lax.broadcasted_iota(jnp.int32, (block, tokens), 1)
-            earlier = (meta_col[part, 1:2] == code) & (below < across)
-            rank += jnp.sum(jnp.where(earlier, 1.0, 0.0), axis=0, keepdims=True)
-            allowed = (meta_col[part, 0:1] == meta_row[0:1, :]) & (across <= below)
-            bias[part, :] = jnp.where(allowed, 0.0, -1e30)
-        slot = jnp.where(code >= 0, code * capacity + rank.astype(jnp.int32), -1)
-        for s in range(0, slots, 128):
-            row = lax.broadcasted_iota(jnp.int32, (128, tokens), 0) + s
-            pick[s : s + 128, :] = jnp.where(row == slot, 1.0, 0.0).astype(jnp.bfloat16)
-
+    rank = jnp.zeros((1, tokens), jnp.float32)
     for b in range(tokens // block):
-        part = slice(b * block, (b + 1) * block)
-        end = (b + 1) * block
-        scores = lax.dot_general(
-            q[0, part, :], k[0, :end, :], (((1,), (1,)), ((), ())), preferred_element_type=jnp.float32
-        )
-        scores = scores * scale + bias[part, :end]
-        raised = jnp.exp(scores - jnp.max(scores, axis=-1, keepdims=True))
-        total = jnp.sum(raised, axis=-1, keepdims=True)
-        mixed = jnp.dot(raised.astype(jnp.bfloat16), v[0, :end, :], preferred_element_type=jnp.float32)
-        attended[part, :] = (mixed / total).astype(jnp.bfloat16)
-    out[...] = jnp.dot(pick[...], attended[...], preferred_element_type=jnp.float32).astype(jnp.bfloat16)
-
-
-def attend(qkv, meta, slots, capacity):
-    _, tokens, hw = qkv.shape
-    part = lambda which: pl.BlockSpec((1, tokens, HD), lambda h: (which, 0, h))
+        below = lax.broadcasted_iota(jnp.int32, (block, tokens), 0) + b * block
+        across = lax.broadcasted_iota(jnp.int32, (block, tokens), 1)
+        earlier = (meta_col[b * block : (b + 1) * block, 1:2] == code) & (below < across)
+        rank += jnp.sum(jnp.where(earlier, 1.0, 0.0), axis=0, keepdims=True)
+    slot_row[...] = jnp.where(code >= 0, code * capacity + rank.astype(jnp.int32), -1)
+
+    pl.semaphore_wait(barrier, peers + ring - 1)
+    for n in range(groups):
+        weight_copy(n).wait()
+    residual_copy().wait()
+
+    def chosen(j):
+        parts = []
+        for k in range(per_chunk):
+            row = lax.broadcasted_iota(jnp.int32, (capacity, tokens), 0)
+            parts.append((row + target(j * per_chunk + k) * capacity) == slot_row[...])
+        return jnp.concatenate(parts, axis=0) if per_chunk > 1 else parts[0]
+
+    def as_pick(hit):
+        return jnp.where(hit, 1.0, 0.0).astype(jnp.bfloat16)
+
+    def attend(j):
+        hit = chosen(j)
+        places = lax.broadcasted_iota(jnp.int32, (rows, tokens), 1)
+        weight = jnp.where(hit, 1.0, 0.0)
+        filled = jnp.sum(weight, axis=-1, keepdims=True)
+        place = jnp.sum(jnp.where(hit, places, 0).astype(jnp.float32), axis=-1, keepdims=True)
+        documents = meta_row[0:1, :].astype(jnp.float32)
+        document = jnp.sum(jnp.where(hit, documents, 0.0), axis=-1, keepdims=True)
+        allowed = (document == documents) & (places.astype(jnp.float32) <= place)
+        bias = jnp.where(allowed, 0.0, -1e30)
+        queries = jnp.dot(
+            weight.astype(jnp.bfloat16), qkv[0], preferred_element_type=jnp.float32
+        ).astype(jnp.bfloat16)
+        heads = []
+        for h in range(inner // HD):
+            lanes = slice(h * HD, (h + 1) * HD)
+            scores = lax.dot_general(
+                queries[:, lanes], qkv[1, :, lanes], (((1,), (1,)), ((), ())),
+                preferred_element_type=jnp.float32,
+            )
+            scores = scores * scale + bias
+            raised = jnp.exp(scores - jnp.max(scores, axis=-1, keepdims=True))
+            total = jnp.sum(raised, axis=-1, keepdims=True)
+            mixed = jnp.dot(
+                raised.astype(jnp.bfloat16), qkv[2, :, lanes], preferred_element_type=jnp.float32
+            )
+            heads.append((mixed * (filled / total)).astype(jnp.bfloat16))
+        return jnp.concatenate(heads, axis=1)
+
+    def multiply(attended, n):
+        return jnp.dot(attended, wbuf[n], preferred_element_type=jnp.float32).astype(jnp.bfloat16)
+
+    def step(s, carry):
+        @pl.when(s < chunks)
+        def _():
+            attended = attend(s)
+            for r in range(ring):
+                pair_send[s, r] = multiply(attended, x_to(r) * 2 + 1 - core)
+            pair_copy(s).start()
+            for r in range(ring):
+                pair_own[s, r] = multiply(attended, x_to(r) * 2 + core)
+            pair_copy(s).wait_recv()
+            for r in range(1, ring):
+                total = pair_own[s, r].astype(jnp.float32) + pair_recv[s, r].astype(jnp.float32)
+                x_send[s, r - 1] = total.astype(jnp.bfloat16)
+                x_copy(s, r).start()
+            kept = jnp.dot(as_pick(chosen(s)), residual[...], preferred_element_type=jnp.float32)
+            acc[s] = (
+                kept + pair_own[s, 0].astype(jnp.float32) + pair_recv[s, 0].astype(jnp.float32)
+            )
+
+        @pl.when(s >= LAG)
+        def _():
+            j = s - LAG
+            total = acc[j]
+            for r in range(1, ring):
+                x_copy(j, r).wait_recv()
+                total += x_recv[j, r - 1].astype(jnp.float32)
+            updated[j] = total.astype(jnp.bfloat16)
+            for k in range(per_chunk - 1):
+                row_copy(j, k).start()
+
+            @pl.when(j < chunks - 1)
+            def _():
+                row_copy(j, per_chunk - 1).start()
+
+        return carry
+
+    lax.fori_loop(0, chunks + LAG, step, 0)
+    own_copy().start()
+
+    def drain(j, carry):
+        pair_copy(j).wait_send()
+        for r in range(1, ring):
+            x_copy(j, r).wait_send()
+        for k in range(per_chunk - 1):
+            row_copy(j, k).wait()
+
+        @pl.when(j < chunks - 1)
+        def _():
+            row_copy(j, per_chunk - 1).wait()
+
+        return carry
+
+    lax.fori_loop(0, chunks, drain, 0)
+    own_copy().wait()
+
+
+def finish(qkv, meta, hidden, w_out, peers, groups):
+    _, tokens, inner = qkv.shape
+    slots = 3 * tokens // 4
+    feature_slice = w_out.shape[1] // groups
+    chunks = min(CHUNKS, peers)
+    rows = slots // chunks
+    ring = groups // 2
+    dma = pltpu.SemaphoreType.DMA
+    bf16 = jnp.bfloat16
+    vmem = pl.BlockSpec(memory_space=VMEM)
+    far = pl.BlockSpec(memory_space=ANY)
+    per_chunk = peers // chunks
     return pl.pallas_call(
-        functools.partial(attention_kernel, capacity),
-        grid=(hw // HD,),
-        out_shape=(
-            jax.ShapeDtypeStruct((slots, hw), jnp.bfloat16),
-            jax.ShapeDtypeStruct((slots, tokens), jnp.bfloat16),
+        functools.partial(tail_kernel, peers, groups, per_chunk),
+        out_shape=jax.ShapeDtypeStruct((slots, feature_slice), bf16),
+        in_specs=[vmem, vmem, vmem, far, far],
+        out_specs=far,
+        scratch_shapes=[
+            VMEM((groups, inner, feature_slice), bf16),
+            VMEM((tokens, feature_slice), bf16),
+            VMEM((1, tokens), jnp.int32),
+            VMEM((chunks, ring, rows, feature_slice), bf16),
+            VMEM((chunks, ring, rows, feature_slice), bf16),
+            VMEM((chunks, ring, rows, feature_slice), bf16),
+            VMEM((chunks, ring - 1, rows, feature_slice), bf16),
+            VMEM((chunks, ring - 1, rows, feature_slice), bf16),
+            VMEM((chunks, rows, feature_slice), jnp.float32),
+            VMEM((chunks, rows, feature_slice), bf16),
+            dma((groups,)),
+            dma,
+            dma((chunks,)),
+            dma((chunks,)),
+            dma((chunks, ring - 1)),
+            dma((chunks, ring - 1)),
+            dma((chunks, per_chunk)),
+            dma((chunks, per_chunk)),
+            dma,
+        ],
+        compiler_params=pltpu.CompilerParams(
+            collective_id=0, has_side_effects=True, vmem_limit_bytes=60 * 2**20
         ),
-        in_specs=[
-            part(0),
-            part(1),
-            part(2),
-            pl.BlockSpec((2, tokens), lambda h: (0, 0)),
-            pl.BlockSpec((tokens, 2), lambda h: (0, 0)),
-        ],
-        out_specs=(
-            pl.BlockSpec((slots, HD), lambda h: (0, h)),
-            pl.BlockSpec((slots, tokens), lambda h: (0, 0)),
-        ),
-        scratch_shapes=[VMEM((tokens, tokens), jnp.float32), VMEM((tokens, HD), jnp.bfloat16)],
-        compiler_params=pltpu.CompilerParams(vmem_limit_bytes=48 * 2**20),
-        name="attend",
-    )(qkv, qkv, qkv, meta, meta.T)
+        name="finish",
+    )(qkv, meta, meta.T, hidden, w_out)
 
 
 def body(hidden, exit_depth, seq_ids, dest, norm_gain, w_query, w_key, w_value, w_out):
     peers = lax.axis_size("dp")
     groups = lax.axis_size("mp")
-    tokens, width = hidden.shape
-    slots = 3 * tokens // 4
-    capacity = slots // peers
-    feature_slice = width // groups
     meta = jnp.stack([seq_ids, jnp.where(exit_depth == 3, dest, -1)])
     qkv = project(hidden, norm_gain, w_query, w_key, w_value)
-    attended, pick = attend(qkv, meta, slots, capacity)
-    own_hidden = lax.dynamic_slice_in_dim(
-        hidden, lax.axis_index("mp") * feature_slice, feature_slice, 1
-    )
-    partial_value = jnp.dot(attended, w_out, preferred_element_type=jnp.float32).astype(jnp.bfloat16)
-    own_features = jnp.dot(pick, own_hidden, preferred_element_type=jnp.float32)
-    summed = lax.psum_scatter(partial_value, "mp", scatter_dimension=1, tiled=True).astype(
-        jnp.float32
-    )
-    updated = (own_features + summed).astype(jnp.bfloat16)
-    return lax.all_to_all(updated, "dp", split_axis=0, concat_axis=0, tiled=True)
+    return finish(qkv, meta, hidden, w_out, peers, groups)
 
 
 def solution(mesh):

time: 211 us -> 119 us (0.56)
  waiting for transfers between devices: 70.9 us -> 0 us
  Pallas kernels: 58 us -> 110 us
  blocking collectives: 50.9 us -> 0 us
  between operations: 13.4 us -> 0.04 us
  matrix products: 13 us -> 0 us
  local copies, waits for them, and re-layouts: 2.82 us -> 5.29 us
    reduce_scatter x1 -> x0, waiting for transfers between devices: 70.8 us -> none  [body(): lax.psum_scatter(partial_value, 'mp', scatter_dimension=1, tiled=True)]
    pallas_call x1, Pallas kernels: 15.6 us -> 68.1 us  [finish(): pl.pallas_call(functools.partial(tail_kernel, peers, groups, per_chunk),...]
    all_to_all x1 -> x0, blocking collectives: 50.9 us -> none  [body(): lax.all_to_all(updated, 'dp', split_axis=0, concat_axis=0, tiled=True)]
    dot_general x2 -> x0, matrix products: 13 us -> none  [the longest x1 8.45 us: body(): jnp.dot(attended, w_out, preferred_element_type=jnp.float32)]
  transfers between devices with their start and end apart: 1 -> 0, of which waited for: 1 -> 0; matrix products, arithmetic and copies ran while one was open for 0% -> 0% of each run, Pallas kernels for 0% -> 0%
where the time goes in v3:
time: 119 us; the launch traced here: 117 us
  Pallas kernels  110 us (92%)
  local copies, waits for them, and re-layouts  5.29 us (4%)
  other arithmetic  1.4 us (1%)
    pallas_call x1, Pallas kernels, finish(): pl.pallas_call(functools.partial(tail_kernel, peers, groups, per_chunk),...  68.1 us
    pallas_call x1, Pallas kernels, project(): pl.pallas_call(functools.partial(qkv_kernel, blocks, bn, rows), grid=(3 *...  42.3 us
    unnamed x3, local copies, waits for them, and re-layouts  2.95 us

profile of v3, /device:TPU:0, one launch (start us, length us, event | category | flops | bytes accessed | tf_op | source)
XLA Modules:
  0.0 117.2 jit_solution(5121511732180553645)
XLA Ops:
  0.0 0.7 compare_select_fusion
  0.7 0.7 pad_add_fusion.meta_row
  1.4 0.0 copy-start
  1.4 1.3 %reshape.3.gain = bf16[1,5120]{1,0:T(2,128)(2,1)} reshape(bf16[5120]{0:T(1024)(128)(2,1)} %param.15) | data formatting | bytes 20480 | tf_op jit(solution)/shard_map/reshape | solution.py:128
  2.7 1.0 copy.16
  3.8 42.3 %qkv.1 = bf16[3,1024,768]{2,1,0:T(8,128)(2,1)} custom-call(bf16[1024,5120]{1,0:T(8,128)(2,1)} %hidden.3, bf16[1,5120]{1,0:T(2,128)(2,1)} %reshape.3.gain, bf16[5120,768]{1,0:T(8,128)(2,1)} %wq.1, bf16[5120,768]{1,0:T(8,128)(2,1)} %wk.1, bf16[5120,768]{1,0:T(8,128)(2,1)} %wv.1, f32[1024,128]{1,0:T(8,128)} %constant.8.clone.cosine, f32[1024,128]{1,0:T(8,128)} %constant.9.clone.sine), custom_call_target="tpu_custom_call" | custom-call | tf_op jit(solution)/shard_map/qkv/pallas_call | solution.py:105
  46.1 0.0 copy-done
  46.1 68.1 %finish.1 = bf16[768,1280]{1,0:T(8,128)(2,1)} custom-call(bf16[3,1024,768]{2,1,0:T(8,128)(2,1)} %qkv.1, s32[2,1024]{1,0:T(2,128)} %copy-done, s32[1024,2]{1,0:T(8,128)} %bitcast.3, bf16[1024,5120]{1,0:T(8,128)(2,1)} %hidden.3, bf16[768,5120]{1,0:T(8,128)(2,1)} %w_out.1), custom_call_target="tpu_custom_call" | custom-call | tf_op jit(solution)/shard_map/finish/pallas_call | solution.py:329
  114.3 2.9 %copy.18 = bf16[768,1280]{1,0:T(8,128)(2,1)} copy(bf16[768,1280]{1,0:T(8,128)(2,1)} %finish.1) | data formatting | bytes 3932160
Async XLA Ops:
  1.4 44.7 %copy-start = (s32[2,1024]{1,0:T(2,128)}, s32[2,1024]{1,0:T(2,128)S(1)}, u32[]{:S(2)}) copy-start(s32[2,1024]{1,0:T(2,128)S(1)} %pad_add_fusion.meta_row) | copy-start | bytes 24580

commit v4 on v3

--- a/solution.py
+++ b/solution.py
@@ -64,7 +64,7 @@
             part = pl.ds(pl.multiple_of(r * rows, rows), rows)
             x = held[part, :].astype(jnp.float32)
             mean_square = jnp.mean(x * x, axis=-1, keepdims=True)
-            y = x * lax.rsqrt(mean_square + 1e-05) * gain[...].astype(jnp.float32)
+            y = x * lax.rsqrt(mean_square + 1e-05) * gain[...].astype(jnp.float32)[None, :]
             normed[part, :] = y.astype(jnp.bfloat16)
             return carry
 
@@ -108,7 +108,7 @@
         out_shape=jax.ShapeDtypeStruct((3, tokens, hw), jnp.bfloat16),
         in_specs=[
             pl.BlockSpec(memory_space=ANY),
-            whole(1, width),
+            whole(width),
             pl.BlockSpec(memory_space=ANY),
             pl.BlockSpec(memory_space=ANY),
             pl.BlockSpec(memory_space=ANY),
@@ -125,11 +125,11 @@
         ],
         compiler_params=pltpu.CompilerParams(vmem_limit_bytes=60 * 2**20),
         name="qkv",
-    )(hidden, gain.reshape(1, width), wq, wk, wv, cosine, sine)
+    )(hidden, gain, wq, wk, wv, cosine, sine)
 
 
 def tail_kernel(
-    peers, groups, per_chunk, qkv, meta_row, meta_col, hidden, w_out, out,
+    peers, groups, per_chunk, qkv, meta_row, hidden, w_out, out,
     wbuf, residual, slot_row, pair_send, pair_own, pair_recv, x_send, x_recv, acc, updated,
     wsem, rsem, pair_ssem, pair_rsem, x_ssem, x_rsem, row_ssem, row_rsem, own_sem,
 ):
@@ -202,20 +202,16 @@
     pl.semaphore_signal(barrier, inc=1, device_id={"mp": partner}, device_id_type=mesh_id)
 
     code = meta_row[1:2, :]
-    block = 256
-    rank = jnp.zeros((1, tokens), jnp.float32)
-    for b in range(tokens // block):
-        below = lax.broadcasted_iota(jnp.int32, (block, tokens), 0) + b * block
-        across = lax.broadcasted_iota(jnp.int32, (block, tokens), 1)
-        earlier = (meta_col[b * block : (b + 1) * block, 1:2] == code) & (below < across)
-        rank += jnp.sum(jnp.where(earlier, 1.0, 0.0), axis=0, keepdims=True)
+    hot_shape = (max(16, peers), tokens)
+    hot = jnp.where(lax.broadcasted_iota(jnp.int32, hot_shape, 0) == code, 1.0, 0.0)
+    below = lax.broadcasted_iota(jnp.int32, (tokens, tokens), 0)
+    across = lax.broadcasted_iota(jnp.int32, (tokens, tokens), 1)
+    before = jnp.where(below < across, 1.0, 0.0).astype(jnp.bfloat16)
+    count = jnp.dot(hot.astype(jnp.bfloat16), before, preferred_element_type=jnp.float32)
+    rank = jnp.sum(hot * count, axis=0, keepdims=True)
     slot_row[...] = jnp.where(code >= 0, code * capacity + rank.astype(jnp.int32), -1)
 
     pl.semaphore_wait(barrier, peers + ring - 1)
-    for n in range(groups):
-        weight_copy(n).wait()
-    residual_copy().wait()
-
     def chosen(j):
         parts = []
         for k in range(per_chunk):
@@ -262,6 +258,13 @@
         @pl.when(s < chunks)
         def _():
             attended = attend(s)
+
+            @pl.when(s == 0)
+            def _():
+                for n in range(groups):
+                    weight_copy(n).wait()
+                residual_copy().wait()
+
             for r in range(ring):
                 pair_send[s, r] = multiply(attended, x_to(r) * 2 + 1 - core)
             pair_copy(s).start()
@@ -329,7 +332,7 @@
     return pl.pallas_call(
         functools.partial(tail_kernel, peers, groups, per_chunk),
         out_shape=jax.ShapeDtypeStruct((slots, feature_slice), bf16),
-        in_specs=[vmem, vmem, vmem, far, far],
+        in_specs=[vmem, vmem, far, far],
         out_specs=far,
         scratch_shapes=[
             VMEM((groups, inner, feature_slice), bf16),
@@ -356,7 +359,7 @@
             collective_id=0, has_side_effects=True, vmem_limit_bytes=60 * 2**20
         ),
         name="finish",
-    )(qkv, meta, meta.T, hidden, w_out)
+    )(qkv, meta, hidden, w_out)
 
 
 def body(hidden, exit_depth, seq_ids, dest, norm_gain, w_query, w_key, w_value, w_out):

time: 119 us -> 115 us (0.966)
  local copies, waits for them, and re-layouts: 5.29 us -> 2.94 us
  Pallas kernels: 110 us -> 108 us
    pallas_call x1, Pallas kernels: 68.1 us -> 65.9 us  [finish(): pl.pallas_call(functools.partial(tail_kernel, peers, groups, per_chunk),...]
    reshape x1 -> x0, local copies, waits for them, and re-layouts: 1.31 us -> none  [project(): gain.reshape(1, width)]
    unnamed x3 -> x1, local copies, waits for them, and re-layouts: 2.95 us -> 2.94 us
where the time goes in v4:
time: 115 us; the launch traced here: 113 us
  Pallas kernels  108 us (94%)
  local copies, waits for them, and re-layouts  2.94 us (3%)
  other arithmetic  2 us (2%)
    pallas_call x1, Pallas kernels, finish(): pl.pallas_call(functools.partial(tail_kernel, peers, groups, per_chunk),...  65.9 us
    pallas_call x1, Pallas kernels, project(): pl.pallas_call(functools.partial(qkv_kernel, blocks, bn, rows), grid=(3 *...  42.4 us
    unnamed x1, local copies, waits for them, and re-layouts  2.94 us

profile of v4, /device:TPU:0, one launch (start us, length us, event | category | flops | bytes accessed | tf_op | source)
XLA Modules:
  0.0 113.3 jit_solution(10300850071885550348)
XLA Ops:
  0.0 0.7 compare_select_fusion
  0.7 1.3 %pad_add_fusion.meta_row = s32[2,1024]{1,0:T(2,128)} fusion(s32[1,1024]{1,0:T(1,128)S(1)} %bitcast.2, s32[1,1024]{1,0:T(1,128)} %bitcast.3), kind=kLoop, calls=%fused_computation | loop fusion | flops 2048 | bytes 16384 | tf_op jit(solution)/shard_map/stack | solution.py:368
  2.0 42.4 %qkv.1 = bf16[3,1024,768]{2,1,0:T(8,128)(2,1)} custom-call(bf16[1024,5120]{1,0:T(8,128)(2,1)} %hidden.3, bf16[5120]{0:T(1024)(128)(2,1)} %gain.1, bf16[5120,768]{1,0:T(8,128)(2,1)} %wq.1, bf16[5120,768]{1,0:T(8,128)(2,1)} %wk.1, bf16[5120,768]{1,0:T(8,128)(2,1)} %wv.1, f32[1024,128]{1,0:T(8,128)} %constant.8.clone.cosine, f32[1024,128]{1,0:T(8,128)} %constant.9.clone.sine), custom_call_target="tpu_custom_call" | custom-call | tf_op jit(solution)/shard_map/qkv/pallas_call | solution.py:105
  44.4 65.9 %finish.1 = bf16[768,1280]{1,0:T(8,128)(2,1)} custom-call(bf16[3,1024,768]{2,1,0:T(8,128)(2,1)} %qkv.1, s32[2,1024]{1,0:T(2,128)} %pad_add_fusion.meta_row, bf16[1024,5120]{1,0:T(8,128)(2,1)} %hidden.3, bf16[768,5120]{1,0:T(8,128)(2,1)} %w_out.1), custom_call_target="tpu_custom_call" | custom-call | tf_op jit(solution)/shard_map/finish/pallas_call | solution.py:332
  110.3 2.9 %copy.13 = bf16[768,1280]{1,0:T(8,128)(2,1)} copy(bf16[768,1280]{1,0:T(8,128)(2,1)} %finish.1) | data formatting | bytes 3932160
